TPU v7x, 32 devices: a whole 2x2x4 slice. The times are simulated.
32 devices in a mesh: row: 4 (over y, x), col: 8 (over z, core).
Axes of the slice: x: 2, y: 2, z: 4, core: 2. Of those that a mesh axis runs over, the one named last changes fastest.
Arguments:
- frame: bfloat16 [128, 256, 256], P('row', 'col'), may hold values from -6 to 6
- gain_attn: float32 [2, 256], replicated, may hold values from 0.1 to 1.9
- w_qkv: bfloat16 [2, 256, 768], replicated, may hold values from -2 to 2
- w_out: bfloat16 [2, 256, 256], replicated, may hold values from -1 to 1
- gain_mlp: float32 [2, 256], replicated, may hold values from 0.1 to 1.9
- w_up: bfloat16 [2, 256, 1024], replicated, may hold values from -0.375 to 0.375
- w_down: bfloat16 [2, 1024, 256], replicated, may hold values from -0.1875 to 0.1875
Outputs:
- result: bfloat16 [128, 256, 256], P('row', 'col')
All inputs are finite; a program needn't handle non-finite values.
Results may differ from a plain program's by a relative error of at most 0.014.
The roundings to bfloat16 on the way count: a program that leaves them out, or rounds other values in their place, can miss the bound.
Values may be sent and summed in bfloat16 or wider, within the bound.
A program may use at most 128 MiB of HBM per device.

v0:
```python
import functools
import math

import jax
import jax.numpy as jnp
from jax import lax
from jax.experimental import pallas as pl
from jax.experimental.pallas import tpu as pltpu
from jax.sharding import PartitionSpec as P

D = 256
HEADS = 8
SW = 8
LAYERS = 2
HALF = HEADS // 2
HD = D // HEADS
EPS = 1e-05
SCALE = HD**-0.5 * math.log2(math.e)
REACH = 96.0
ONES = 16


def normalize(floats, gain):
    center = floats - jnp.mean(floats, axis=-1, keepdims=True)
    spread = jnp.mean(center * center, axis=-1, keepdims=True)
    return center * lax.rsqrt(spread + EPS) * gain


def project(normed, wt_ref, sent_a, sent_d):
    rows, bands, _, _ = normed.shape
    for band in range(rows // SW):
        tokens = normed[band * SW : (band + 1) * SW].reshape(-1, D).astype(jnp.bfloat16)
        qkv = lax.dot_general(
            wt_ref[: HALF * 3 * HD], tokens, (((1,), (1,)), ((), ())), preferred_element_type=jnp.float32
        ).astype(jnp.bfloat16)
        sent_a[band * HALF : (band + 1) * HALF] = qkv.reshape(HALF, 3 * HD, -1)
    for band in range(bands):
        tokens = normed[:, band].reshape(-1, D).astype(jnp.bfloat16)
        qkv = lax.dot_general(
            wt_ref[HALF * 3 * HD :], tokens, (((1,), (1,)), ((), ())), preferred_element_type=jnp.float32
        ).astype(jnp.bfloat16)
        sent_d[band * HALF : (band + 1) * HALF] = qkv.reshape(HALF, 3 * HD, -1)


def first_kernel(x_ref, gain_ref, wt_ref, sent_a, sent_d, normed):
    rows, cols, _ = x_ref.shape
    for band in range(rows // SW):
        part = slice(band * SW, (band + 1) * SW)
        floats = x_ref[part].reshape(-1, D).astype(jnp.float32)
        normed[part] = normalize(floats, gain_ref[...]).reshape(SW, cols // SW, SW, D)
    project(normed, wt_ref, sent_a, sent_d)


def rest(x_ref, heads_a, heads_d, w_out, gain_mlp, w_up, w_down, y_ref, mixed, normed, gain):
    rows, cols, _ = x_ref.shape
    bands = cols // SW
    flip = (((0,), (0,)), ((), ()))
    for band in range(bands):
        heads = heads_d[band * HALF : (band + 1) * HALF].reshape(HALF * HD, -1)
        part = lax.dot_general(heads, w_out[HALF * HD :], flip, preferred_element_type=jnp.float32)
        mixed[:, band] = part.reshape(rows, SW, D)
    for band in range(rows // SW):
        here = slice(band * SW, (band + 1) * SW)
        heads = heads_a[band * HALF : (band + 1) * HALF].reshape(HALF * HD, -1)
        part = lax.dot_general(heads, w_out[: HALF * HD], flip, preferred_element_type=jnp.float32)
        total = x_ref[here].reshape(-1, D).astype(jnp.float32) + (part + mixed[here].reshape(-1, D))
        normed2 = normalize(total, gain_mlp[...]).astype(jnp.bfloat16)
        up = jnp.dot(normed2, w_up[...], preferred_element_type=jnp.float32)
        hidden = jax.nn.gelu(up, approximate=True).astype(jnp.bfloat16)
        final = total + jnp.dot(hidden, w_down[...], preferred_element_type=jnp.float32)
        final = final.astype(jnp.bfloat16)
        y_ref[here] = final.reshape(SW, cols, D)
        if normed is not None:
            normed[here] = normalize(final.astype(jnp.float32), gain[...]).reshape(SW, bands, SW, D)


def middle_kernel(
    x_ref, heads_a, heads_d, w_out, gain_mlp, w_up, w_down, gain, wt_ref, y_ref, sent_a, sent_d, mixed, normed
):
    rest(x_ref, heads_a, heads_d, w_out, gain_mlp, w_up, w_down, y_ref, mixed, normed, gain)
    project(normed, wt_ref, sent_a, sent_d)


def last_kernel(x_ref, heads_a, heads_d, w_out, gain_mlp, w_up, w_down, y_ref, mixed):
    rest(x_ref, heads_a, heads_d, w_out, gain_mlp, w_up, w_down, y_ref, mixed, None, None)


def attend_kernel(got_ref, out_ref, keys, vals, queries):
    sources, items, _, width = got_ref.shape

    @pl.loop(0, items)
    def _(item):
        top_q = jnp.zeros((1, width), jnp.float32)
        top_k = jnp.zeros((1, width), jnp.float32)
        for src in range(sources):
            q = got_ref[src, item, :HD].astype(jnp.float32) * SCALE
            high = q.astype(jnp.bfloat16)
            low = (q - high.astype(jnp.float32)).astype(jnp.bfloat16)
            queries[src] = jnp.concatenate([high, low], axis=0)
            k = got_ref[src, item, HD : 2 * HD]
            keys[src * width : (src + 1) * width] = jnp.concatenate([k, k], axis=0).T
            kf = k.astype(jnp.float32)
            vals[src, :HD] = got_ref[src, item, 2 * HD :]
            vals[src, HD:] = jnp.ones((ONES, width), jnp.bfloat16)
            top_q = jnp.maximum(top_q, jnp.sum(q * q, axis=0, keepdims=True))
            top_k = jnp.maximum(top_k, jnp.sum(kf * kf, axis=0, keepdims=True))
        reach = jnp.max(top_q) * jnp.max(top_k)
        narrow = reach < REACH * REACH

        def scores(src, q):
            return jnp.dot(keys[src * width : (src + 1) * width], q, preferred_element_type=jnp.float32)

        def store(block, total):
            out_ref[block, item] = (total[:HD] / total[HD : HD + 1]).astype(jnp.bfloat16)

        @pl.when(narrow)
        def _():
            @pl.loop(0, sources)
            def _(block):
                q = queries[block]
                total = jnp.zeros((HD + ONES, width), jnp.float32)
                for src in range(sources):
                    probs = jnp.exp2(scores(src, q)).astype(jnp.bfloat16)
                    total += jnp.dot(vals[src], probs, preferred_element_type=jnp.float32)
                store(block, total)

        @pl.when(jnp.logical_not(narrow))
        def _():
            @pl.loop(0, sources)
            def _(block):
                q = queries[block]
                top = jnp.full((1, width), -jnp.inf, jnp.float32)
                for src in range(sources):
                    top = jnp.maximum(top, jnp.max(scores(src, q), axis=0, keepdims=True))
                total = jnp.zeros((HD + ONES, width), jnp.float32)
                for src in range(sources):
                    probs = jnp.exp2(scores(src, q) - top).astype(jnp.bfloat16)
                    total += jnp.dot(vals[src], probs, preferred_element_type=jnp.float32)
                store(block, total)


VM = pl.BlockSpec(memory_space=pltpu.VMEM)


def call(kernel, outs, scratch, *args):
    return pl.pallas_call(
        kernel,
        out_shape=outs,
        in_specs=[VM] * len(args),
        out_specs=jax.tree.map(lambda _: VM, outs),
        scratch_shapes=scratch,
    )(*args)


def attend(got):
    sources, items, _, width = got.shape
    return call(
        attend_kernel,
        jax.ShapeDtypeStruct((sources, items, HD, width), jnp.bfloat16),
        [
            pltpu.VMEM((sources * width, 2 * HD), jnp.bfloat16),
            pltpu.VMEM((sources, HD + ONES, width), jnp.bfloat16),
            pltpu.VMEM((sources, 2 * HD, width), jnp.bfloat16),
        ],
        got,
    )


def exchange(array, axis):
    count = lax.axis_size(axis)
    split = array.reshape(count, -1, *array.shape[-2:])
    return lax.all_to_all(split, axis, split_axis=0, concat_axis=0, tiled=True)


def shards(frame, gain_attn, w_qkv, w_out, gain_mlp, w_up, w_down):
    rows, cols, _ = frame.shape
    items_a = rows // SW * HALF
    items_d = cols // SW * HALF
    wt = w_qkv.reshape(LAYERS, D, 3, HEADS, HD).transpose(0, 3, 2, 4, 1).reshape(LAYERS, 3 * D, D)
    sent = (
        jax.ShapeDtypeStruct((items_a, 3 * HD, SW * cols), jnp.bfloat16),
        jax.ShapeDtypeStruct((items_d, 3 * HD, SW * rows), jnp.bfloat16),
    )
    scratch = pltpu.VMEM((rows, cols // SW, SW, D), jnp.float32)
    shape = jax.ShapeDtypeStruct(frame.shape, jnp.bfloat16)
    state = frame
    sent_a, sent_d = call(first_kernel, sent, [scratch], frame, gain_attn[:1], wt[0])
    for layer in range(LAYERS):
        heads_d = exchange(attend(exchange(sent_d, "row")), "row").reshape(items_d, HD, -1)
        heads_a = exchange(attend(exchange(sent_a, "col")), "col").reshape(items_a, HD, -1)
        args = (state, heads_a, heads_d, w_out[layer], gain_mlp[layer : layer + 1], w_up[layer], w_down[layer])
        if layer + 1 < LAYERS:
            state, sent_a, sent_d = call(
                middle_kernel,
                (shape,) + sent,
                [scratch, scratch],
                *args,
                gain_attn[layer + 1 : layer + 2],
                wt[layer + 1],
            )
        else:
            state = call(last_kernel, shape, [scratch], *args)
    return state


def solution(mesh):
    placed = (P("row", "col", None), P(), P(), P(), P(), P(), P())
    return jax.shard_map(
        shards, mesh=mesh, in_specs=placed, out_specs=P("row", "col", None), check_vma=False
    )
```

profile of v0, /device:TPU:0, one launch (start us, length us, event | category | flops | bytes accessed | tf_op | source)
XLA Modules:
  0.0 179.6 jit_solution(14611573098448183894)
XLA Ops:
  0.0 1.4 fusion.2
  1.4 1.4 copy.9
  2.8 0.8 copy.10
  3.6 3.1 %shard_map.73 = (bf16[16,96,256]{2,1,0:T(8,128)(2,1)}, bf16[16,96,256]{2,1,0:T(8,128)(2,1)}) custom-call(bf16[32,32,256]{2,1,0:T(8,128)(2,1)} %x_ref.3, f32[1,256]{1,0:T(1,128)} %get-tuple-element.26.gain_ref, bf16[768,256]{1,0:T(8,128)(2,1)} %bitcast.26), custom_call_target="tpu_custom_call" | custom-call | tf_op jit(solution)/shard_map/pallas_call | solution.py:146
  6.7 17.2 %all_to_all.40.got_ref = bf16[4,4,96,256]{3,2,1,0:T(8,128)(2,1)} all-to-all(bf16[4,4,96,256]{3,2,1,0:T(8,128)(2,1)} %bitcast.33), channel_id=1, replica_groups=mesh['row'=4,'col'=8] {'row'}, dimensions={0} | all-to-all | bytes 1572864 | tf_op jit(solution)/shard_map/all_to_all | solution.py:172
  23.8 5.2 %all-to-all-start = ((bf16[8,2,96,256]{3,2,1,0:T(8,128)(2,1)}), bf16[8,2,96,256]{3,2,1,0:T(8,128)(2,1)S(1)}, u32[]{:S(2)}, u32[]{:S(2)}) async-start(bf16[8,2,96,256]{3,2,1,0:T(8,128)(2,1)} %bitcast.3), calls=%async_computation | async-start | bytes 1572864 | tf_op jit(solution)/shard_map/all_to_all | solution.py:172
  29.0 0.8 copy.11
  29.8 1.0 slice_bitcast_fusion.1
  30.9 13.9 %shard_map.75 = bf16[4,4,32,256]{3,2,1,0:T(8,128)(2,1)} custom-call(bf16[4,4,96,256]{3,2,1,0:T(8,128)(2,1)} %all_to_all.40.got_ref), custom_call_target="tpu_custom_call" | custom-call | tf_op jit(solution)/shard_map/pallas_call | solution.py:146
  44.8 5.2 %all-to-all-done.got_ref = bf16[8,2,96,256]{3,2,1,0:T(8,128)(2,1)S(1)} async-done(((bf16[8,2,96,256]{3,2,1,0:T(8,128)(2,1)}), bf16[8,2,96,256]{3,2,1,0:T(8,128)(2,1)S(1)}, u32[]{:S(2)}, u32[]{:S(2)}) %all-to-all-start) | async-done | bytes 786464 | tf_op jit(solution)/shard_map/all_to_all | solution.py:172
  50.0 3.4 %all-to-all-start.3 = ((bf16[4,4,32,256]{3,2,1,0:T(8,128)(2,1)}), bf16[4,4,32,256]{3,2,1,0:T(8,128)(2,1)S(1)}, u32[]{:S(2)}, u32[]{:S(2)}) async-start(bf16[4,4,32,256]{3,2,1,0:T(8,128)(2,1)} %shard_map.75), calls=%async_computation.3 | async-start | bytes 524288 | tf_op jit(solution)/shard_map/all_to_all | solution.py:172
  54.2 21.0 %shard_map.74 = bf16[8,2,32,256]{3,2,1,0:T(8,128)(2,1)} custom-call(bf16[8,2,96,256]{3,2,1,0:T(8,128)(2,1)} %copy-done), custom_call_target="tpu_custom_call" | custom-call | tf_op jit(solution)/shard_map/pallas_call | solution.py:146
  75.9 3.4 %all-to-all-start.1 = ((bf16[8,2,32,256]{3,2,1,0:T(8,128)(2,1)}), bf16[8,2,32,256]{3,2,1,0:T(8,128)(2,1)S(1)}, u32[]{:S(2)}, u32[]{:S(2)}) async-start(bf16[8,2,32,256]{3,2,1,0:T(8,128)(2,1)} %shard_map.74), calls=%async_computation.1 | async-start | bytes 524288 | tf_op jit(solution)/shard_map/all_to_all | solution.py:172
  79.9 1.0 slice_bitcast_fusion
  80.9 8.0 %all-to-all-done.1 = bf16[8,2,32,256]{3,2,1,0:T(8,128)(2,1)S(1)} async-done(((bf16[8,2,32,256]{3,2,1,0:T(8,128)(2,1)}), bf16[8,2,32,256]{3,2,1,0:T(8,128)(2,1)S(1)}, u32[]{:S(2)}, u32[]{:S(2)}) %all-to-all-start.1) | async-done | bytes 262176 | tf_op jit(solution)/shard_map/all_to_all | solution.py:172
  89.6 6.2 %shard_map.76 = (bf16[32,32,256]{2,1,0:T(8,128)(2,1)}, bf16[16,96,256]{2,1,0:T(8,128)(2,1)}, bf16[16,96,256]{2,1,0:T(8,128)(2,1)}) custom-call(bf16[32,32,256]{2,1,0:T(8,128)(2,1)} %x_ref.3, bf16[16,32,256]{2,1,0:T(8,128)(2,1)} %bitcast.29, bf16[16,32,256]{2,1,0:T(8,128)(2,1)} %bitcast.28, bf16[256,256]{1,0:T(8,128)(2,1)} %get-tuple-element.22.w_out, ...), custom_call_target="tpu_custom_call" | custom-call | tf_op jit(solution)/shard_map/pallas_call | solution.py:146
  95.9 15.7 %all_to_all.41.got_ref = bf16[4,4,96,256]{3,2,1,0:T(8,128)(2,1)} all-to-all(bf16[4,4,96,256]{3,2,1,0:T(8,128)(2,1)} %bitcast.32), channel_id=1, replica_groups=mesh['row'=4,'col'=8] {'row'}, dimensions={0} | all-to-all | bytes 1572864 | tf_op jit(solution)/shard_map/all_to_all | solution.py:172
  111.6 3.5 %all-to-all-start.4 = ((bf16[8,2,96,256]{3,2,1,0:T(8,128)(2,1)}), bf16[8,2,96,256]{3,2,1,0:T(8,128)(2,1)S(1)}, u32[]{:S(2)}, u32[]{:S(2)}) async-start(bf16[8,2,96,256]{3,2,1,0:T(8,128)(2,1)} %bitcast.12), calls=%async_computation.4 | async-start | bytes 1572864 | tf_op jit(solution)/shard_map/all_to_all | solution.py:172
  115.2 13.9 %shard_map.78 = bf16[4,4,32,256]{3,2,1,0:T(8,128)(2,1)} custom-call(bf16[4,4,96,256]{3,2,1,0:T(8,128)(2,1)} %all_to_all.41.got_ref), custom_call_target="tpu_custom_call" | custom-call | tf_op jit(solution)/shard_map/pallas_call | solution.py:146
  129.1 7.0 %all-to-all-done.4.got_ref = bf16[8,2,96,256]{3,2,1,0:T(8,128)(2,1)S(1)} async-done(((bf16[8,2,96,256]{3,2,1,0:T(8,128)(2,1)}), bf16[8,2,96,256]{3,2,1,0:T(8,128)(2,1)S(1)}, u32[]{:S(2)}, u32[]{:S(2)}) %all-to-all-start.4) | async-done | bytes 786464 | tf_op jit(solution)/shard_map/all_to_all | solution.py:172
  136.0 3.4 %all-to-all-start.7 = ((bf16[4,4,32,256]{3,2,1,0:T(8,128)(2,1)}), bf16[4,4,32,256]{3,2,1,0:T(8,128)(2,1)S(1)}, u32[]{:S(2)}, u32[]{:S(2)}) async-start(bf16[4,4,32,256]{3,2,1,0:T(8,128)(2,1)} %shard_map.78), calls=%async_computation.7 | async-start | bytes 524288 | tf_op jit(solution)/shard_map/all_to_all | solution.py:172
  139.5 21.0 %shard_map.77 = bf16[8,2,32,256]{3,2,1,0:T(8,128)(2,1)} custom-call(bf16[8,2,96,256]{3,2,1,0:T(8,128)(2,1)} %copy-done.1), custom_call_target="tpu_custom_call" | custom-call | tf_op jit(solution)/shard_map/pallas_call | solution.py:146
  160.5 13.7 %all_to_all.42 = bf16[8,2,32,256]{3,2,1,0:T(8,128)(2,1)} all-to-all(bf16[8,2,32,256]{3,2,1,0:T(8,128)(2,1)} %shard_map.77), channel_id=1, replica_groups=mesh['row'=4,'col'=8] {'col'}, dimensions={0} | all-to-all | bytes 524288 | tf_op jit(solution)/shard_map/all_to_all | solution.py:172
  174.2 5.3 %shard_map.79 = bf16[32,32,256]{2,1,0:T(8,128)(2,1)} custom-call(bf16[32,32,256]{2,1,0:T(8,128)(2,1)} %get-tuple-element.12.x_ref, bf16[16,32,256]{2,1,0:T(8,128)(2,1)} %bitcast.31, bf16[16,32,256]{2,1,0:T(8,128)(2,1)} %bitcast.30, bf16[256,256]{1,0:T(8,128)(2,1)} %get-tuple-element.21.w_out, f32[1,256]{1,0:T(1,128)} %get-tuple-element.23.gain_mlp, ...), custom_call_target="tpu_custom_call" | custom-call | tf_op jit(solution)/shard_map/pallas_call | solution.py:146
  (23 shorter events, 2.8 us)
Async XLA Ops:
  23.8 6.0 %copy-start.5 = (bf16[2,256,1024]{2,1,0:T(8,128)(2,1)S(1)}, bf16[2,256,1024]{2,1,0:T(8,128)(2,1)}, u32[]{:S(2)}) copy-start(bf16[2,256,1024]{2,1,0:T(8,128)(2,1)} %param.12) | copy-start | bytes 3145732
  23.8 26.2 %all-to-all-start = ((bf16[8,2,96,256]{3,2,1,0:T(8,128)(2,1)}), bf16[8,2,96,256]{3,2,1,0:T(8,128)(2,1)S(1)}, u32[]{:S(2)}, u32[]{:S(2)}) async-start(bf16[8,2,96,256]{3,2,1,0:T(8,128)(2,1)} %bitcast.3), calls=%async_computation | async-start | bytes 1572864 | tf_op jit(solution)/shard_map/all_to_all | solution.py:172
  44.8 8.7 %copy-start.7 = (bf16[2,256,256]{2,1,0:T(8,128)(2,1)S(1)}, bf16[2,256,256]{2,1,0:T(8,128)(2,1)}, u32[]{:S(2)}) copy-start(bf16[2,256,256]{2,1,0:T(8,128)(2,1)} %param.10) | copy-start | bytes 786436
  50.0 4.2 %copy-start = (bf16[8,2,96,256]{3,2,1,0:T(8,128)(2,1)}, bf16[8,2,96,256]{3,2,1,0:T(8,128)(2,1)S(1)}, u32[]{:S(2)}) copy-start(bf16[8,2,96,256]{3,2,1,0:T(8,128)(2,1)S(1)} %all-to-all-done.got_ref) | copy-start | bytes 2359300
  50.0 25.2 %all-to-all-start.3 = ((bf16[4,4,32,256]{3,2,1,0:T(8,128)(2,1)}), bf16[4,4,32,256]{3,2,1,0:T(8,128)(2,1)S(1)}, u32[]{:S(2)}, u32[]{:S(2)}) async-start(bf16[4,4,32,256]{3,2,1,0:T(8,128)(2,1)} %shard_map.75), calls=%async_computation.3 | async-start | bytes 524288 | tf_op jit(solution)/shard_map/all_to_all | solution.py:172
  53.4 26.5 %copy-start.6 = (bf16[2,1024,256]{2,1,0:T(8,128)(2,1)S(1)}, bf16[2,1024,256]{2,1,0:T(8,128)(2,1)}, u32[]{:S(2)}) copy-start(bf16[2,1024,256]{2,1,0:T(8,128)(2,1)} %param.13) | copy-start | bytes 3145732
  75.2 4.1 %copy-start.8 = (f32[2,256]{1,0:T(2,128)S(1)}, f32[2,256]{1,0:T(2,128)}, u32[]{:S(2)}) copy-start(f32[2,256]{1,0:T(2,128)} %param.11) | copy-start | bytes 6148
  75.2 0.7 copy-start.2
  75.9 13.1 %all-to-all-start.1 = ((bf16[8,2,32,256]{3,2,1,0:T(8,128)(2,1)}), bf16[8,2,32,256]{3,2,1,0:T(8,128)(2,1)S(1)}, u32[]{:S(2)}, u32[]{:S(2)}) async-start(bf16[8,2,32,256]{3,2,1,0:T(8,128)(2,1)} %shard_map.74), calls=%async_computation.1 | async-start | bytes 524288 | tf_op jit(solution)/shard_map/all_to_all | solution.py:172
  88.9 0.7 copy-start.3
  111.6 24.4 %all-to-all-start.4 = ((bf16[8,2,96,256]{3,2,1,0:T(8,128)(2,1)}), bf16[8,2,96,256]{3,2,1,0:T(8,128)(2,1)S(1)}, u32[]{:S(2)}, u32[]{:S(2)}) async-start(bf16[8,2,96,256]{3,2,1,0:T(8,128)(2,1)} %bitcast.12), calls=%async_computation.4 | async-start | bytes 1572864 | tf_op jit(solution)/shard_map/all_to_all | solution.py:172
  136.0 3.4 %copy-start.1 = (bf16[8,2,96,256]{3,2,1,0:T(8,128)(2,1)}, bf16[8,2,96,256]{3,2,1,0:T(8,128)(2,1)S(1)}, u32[]{:S(2)}) copy-start(bf16[8,2,96,256]{3,2,1,0:T(8,128)(2,1)S(1)} %all-to-all-done.4.got_ref) | copy-start | bytes 2359300
  136.0 24.4 %all-to-all-start.7 = ((bf16[4,4,32,256]{3,2,1,0:T(8,128)(2,1)}), bf16[4,4,32,256]{3,2,1,0:T(8,128)(2,1)S(1)}, u32[]{:S(2)}, u32[]{:S(2)}) async-start(bf16[4,4,32,256]{3,2,1,0:T(8,128)(2,1)} %shard_map.78), calls=%async_computation.7 | async-start | bytes 524288 | tf_op jit(solution)/shard_map/all_to_all | solution.py:172
  160.5 13.7 %copy-start.4 = (bf16[4,4,32,256]{3,2,1,0:T(8,128)(2,1)}, bf16[4,4,32,256]{3,2,1,0:T(8,128)(2,1)S(1)}, u32[]{:S(2)}) copy-start(bf16[4,4,32,256]{3,2,1,0:T(8,128)(2,1)S(1)} %all-to-all-done.7) | copy-start | bytes 786436
where the time goes:
time: 181 us; the launch traced here: 180 us
  Pallas kernels  84.5 us (47%)
  blocking collectives  46.6 us (26%)
  waiting for transfers between devices  20.2 us (11%)
  starting transfers between devices  19 us (10%)
  local copies, waits for them, and re-layouts  9.16 us (5%)
    pallas_call x7, Pallas kernels, call(): pl.pallas_call(kernel, out_shape=outs, in_specs=[VM] * len(args), out_spe...  84.5 us
    all_to_all x3, blocking collectives, exchange(): return lax.all_to_all(split, axis, split_axis=0, concat_axis=0, tiled=True)  46.6 us
    all_to_all x5, waiting for transfers between devices, exchange(): return lax.all_to_all(split, axis, split_axis=0, concat_axis=0, tiled=True)  20.2 us
    all_to_all x5, starting transfers between devices, exchange(): return lax.all_to_all(split, axis, split_axis=0, concat_axis=0, tiled=True)  19 us
  transfers between devices with their start and end apart: 5, of which 3 were waited for; matrix products, arithmetic and copies ran while one was open for 2% of the time, Pallas kernels for 39%

commit v1 on v0

v1 whole, which is shorter than its diff:
```python
import functools
import math

import jax
import jax.numpy as jnp
from jax import lax
from jax.experimental import pallas as pl
from jax.experimental.pallas import tpu as pltpu
from jax.sharding import PartitionSpec as P

D = 256
HEADS = 8
SW = 8
LAYERS = 2
HALF = HEADS // 2
HD = D // HEADS
EPS = 1e-05
SCALE = HD**-0.5 * math.log2(math.e)


def normalize(floats, gain):
    center = floats - jnp.mean(floats, axis=-1, keepdims=True)
    spread = jnp.mean(center * center, axis=-1, keepdims=True)
    return center * lax.rsqrt(spread + EPS) * gain


def project(normed, w_ref, sent_a, sent_d, wt):
    rows, bands, _, _ = normed.shape
    side = HALF * HD
    for part in range(3):
        wt[part] = w_ref[:, part * D : (part + 1) * D].T

    def emit(tokens, first, sent, band):
        tokens = tokens.reshape(-1, D).astype(jnp.bfloat16)
        for part in range(3):
            out = lax.dot_general(
                wt[part, first : first + side],
                tokens,
                (((1,), (1,)), ((), ())),
                preferred_element_type=jnp.float32,
            )
            sent[band * HALF : (band + 1) * HALF, part * HD : (part + 1) * HD] = (
                out.astype(jnp.bfloat16).reshape(HALF, HD, -1)
            )

    for band in range(bands):
        emit(normed[:, band], side, sent_d, band)
    for band in range(rows // SW):
        emit(normed[band * SW : (band + 1) * SW], 0, sent_a, band)


def first_kernel(x_ref, gain_ref, w_ref, sent_a, sent_d, normed, wt):
    rows, cols, _ = x_ref.shape
    for band in range(rows // SW):
        part = slice(band * SW, (band + 1) * SW)
        floats = x_ref[part].reshape(-1, D).astype(jnp.float32)
        normed[part] = normalize(floats, gain_ref[...]).reshape(SW, cols // SW, SW, D)
    project(normed, w_ref, sent_a, sent_d, wt)


def rest(x_ref, heads_a, heads_d, w_out, gain_mlp, w_up, w_down, y_ref, mixed, normed, gain):
    rows, cols, _ = x_ref.shape
    bands = cols // SW
    flip = (((0,), (0,)), ((), ()))
    for band in range(bands):
        heads = heads_d[band * HALF : (band + 1) * HALF].reshape(HALF * HD, -1)
        part = lax.dot_general(heads, w_out[HALF * HD :], flip, preferred_element_type=jnp.float32)
        mixed[:, band] = part.reshape(rows, SW, D)
    for band in range(rows // SW):
        here = slice(band * SW, (band + 1) * SW)
        heads = heads_a[band * HALF : (band + 1) * HALF].reshape(HALF * HD, -1)
        part = lax.dot_general(heads, w_out[: HALF * HD], flip, preferred_element_type=jnp.float32)
        total = x_ref[here].reshape(-1, D).astype(jnp.float32) + (part + mixed[here].reshape(-1, D))
        normed2 = normalize(total, gain_mlp[...]).astype(jnp.bfloat16)
        up = jnp.dot(normed2, w_up[...], preferred_element_type=jnp.float32)
        hidden = jax.nn.gelu(up, approximate=True).astype(jnp.bfloat16)
        final = total + jnp.dot(hidden, w_down[...], preferred_element_type=jnp.float32)
        final = final.astype(jnp.bfloat16)
        y_ref[here] = final.reshape(SW, cols, D)
        if normed is not None:
            normed[here] = normalize(final.astype(jnp.float32), gain[...]).reshape(SW, bands, SW, D)


def middle_kernel(
    x_ref, heads_a, heads_d, w_out, gain_mlp, w_up, w_down, gain, w_ref, y_ref, sent_a, sent_d, mixed, normed, wt
):
    rest(x_ref, heads_a, heads_d, w_out, gain_mlp, w_up, w_down, y_ref, mixed, normed, gain)
    project(normed, w_ref, sent_a, sent_d, wt)


def last_kernel(x_ref, heads_a, heads_d, w_out, gain_mlp, w_up, w_down, y_ref, mixed):
    rest(x_ref, heads_a, heads_d, w_out, gain_mlp, w_up, w_down, y_ref, mixed, None, None)


def wrap(index, count):
    return lax.rem(index + count, count)


class Stream:
    def __init__(self, axis, sent, heads, got, outs, keys, vals, queries, board, tops, sems):
        self.axis, self.sent, self.heads, self.got, self.outs = axis, sent, heads, got, outs
        self.keys, self.vals, self.queries, self.board, self.tops = keys, vals, queries, board, tops
        self.send_in, self.recv_in, self.send_out, self.recv_out, self.local = sems
        self.count, self.items, _, self.width = got.shape
        self.me = lax.axis_index(axis)
        self.units = self.count * self.items

    def greet(self, barrier):
        for step in range(1, self.count):
            pl.semaphore_signal(barrier, inc=1, device_id={self.axis: wrap(self.me + step, self.count)})

    def inward(self, item, step):
        target = wrap(self.me + step, self.count)
        return pltpu.make_async_remote_copy(
            src_ref=self.sent.at[target, item],
            dst_ref=self.got.at[step, item],
            send_sem=self.send_in.at[item, step],
            recv_sem=self.recv_in.at[item, step],
            device_id={self.axis: target},
        )

    def outward(self, item, step):
        return pltpu.make_async_remote_copy(
            src_ref=self.outs.at[step, item],
            dst_ref=self.heads.at[self.me, item],
            send_sem=self.send_out.at[item, step],
            recv_sem=self.recv_out.at[item, step],
            device_id={self.axis: wrap(self.me - step, self.count)},
        )

    def own(self):
        return pltpu.make_async_copy(self.sent.at[self.me], self.got.at[0], self.local)

    def start(self, item):
        for step in range(1, self.count):
            self.inward(item, step).start()

    def prepare(self, item):
        for step in range(1, self.count):
            self.inward(item, step).wait_recv()
        slot = lax.rem(item, 2)
        for src in range(self.count):
            q = self.got[src, item, :HD].astype(jnp.float32) * SCALE
            high = q.astype(jnp.bfloat16)
            low = (q - high.astype(jnp.float32)).astype(jnp.bfloat16)
            self.queries[src] = jnp.concatenate([high, low], axis=0)
            k = self.got[src, item, HD : 2 * HD]
            self.keys[src * self.width : (src + 1) * self.width] = jnp.concatenate([k, k], axis=0).T
            self.vals[slot, src] = self.got[src, item, 2 * HD :]

    def score(self, unit):
        slot = lax.rem(unit, 2)
        q = self.queries[lax.rem(unit, self.count)]
        tops = []
        for src in range(self.count):
            here = slice(src * self.width, (src + 1) * self.width)
            scores = jnp.dot(self.keys[here], q, preferred_element_type=jnp.float32)
            self.board[slot, here] = scores
            tops.append(jnp.max(scores.reshape(-1, 8, self.width), axis=0))
        self.tops[slot] = jnp.max(functools.reduce(jnp.maximum, tops), axis=0, keepdims=True)

    def finish(self, unit):
        slot = lax.rem(unit, 2)
        item, block = unit // self.count, lax.rem(unit, self.count)
        top = self.tops[slot]
        sums, total = 0.0, 0.0
        for src in range(self.count):
            here = slice(src * self.width, (src + 1) * self.width)
            probs = jnp.exp2(self.board[slot, here] - top)
            sums += jnp.sum(probs.reshape(-1, 8, self.width), axis=0)
            total += jnp.dot(
                self.vals[lax.rem(item, 2), src], probs.astype(jnp.bfloat16), preferred_element_type=jnp.float32
            )
        result = (total / jnp.sum(sums, axis=0, keepdims=True)).astype(jnp.bfloat16)
        self.outs[block, item] = result

    def deliver(self, unit):
        item, block = unit // self.count, lax.rem(unit, self.count)

        @pl.when(block == 0)
        def _():
            self.heads[self.me, item] = self.outs[0, item]

        @pl.when(block != 0)
        def _():
            self.outward(item, block).start()

    def run(self):
        self.prepare(0)
        self.score(0)

        @pl.loop(0, self.units - 1)
        def _(unit):
            after = unit + 1

            @pl.when(lax.rem(after, self.count) == 0)
            def _():
                self.prepare(after // self.count)

            self.score(after)
            self.finish(unit)

            @pl.when(unit > 0)
            def _():
                self.deliver(unit - 1)

        self.finish(self.units - 1)
        if self.units > 1:
            self.deliver(self.units - 2)
        self.deliver(self.units - 1)

    def drain(self):
        for item in range(self.items):
            for step in range(1, self.count):
                self.inward(item, step).wait_send()
                self.outward(item, step).wait()


def layer_kernel(
    sent_a, sent_d, heads_a, heads_d, got_a, got_d, outs_a, outs_d, keys, vals, queries, board, tops, *sems
):
    def stream(axis, sent, heads, got, outs, sems):
        count, _, _, width = got.shape
        return Stream(
            axis,
            sent,
            heads,
            got,
            outs,
            keys.at[: count * width],
            vals.at[:, :count],
            queries.at[:count],
            board.at[:, : count * width],
            tops,
            sems,
        )

    across = stream("col", sent_a, heads_a, got_a, outs_a, sems[:5])
    down = stream("row", sent_d, heads_d, got_d, outs_d, sems[5:])
    barrier = pltpu.get_barrier_semaphore()
    across.greet(barrier)
    down.greet(barrier)
    pl.semaphore_wait(barrier, across.count + down.count - 2)
    for item in range(down.items):
        down.start(item)
        if item == 0:
            across.start(item)
    for item in range(1, across.items):
        across.start(item)
    across.own().start()
    down.own().start()
    across.own().wait()
    down.own().wait()
    down.run()
    across.run()
    down.drain()
    across.drain()


VM = pl.BlockSpec(memory_space=pltpu.VMEM)


def call(kernel, outs, scratch, *args, params=None):
    def spec(arg):
        if not isinstance(arg, tuple):
            return VM
        array, layer = arg
        rest = array.shape[1:]
        return pl.BlockSpec((None,) + rest, lambda i: (layer,) + (0,) * len(rest))

    return pl.pallas_call(
        kernel,
        out_shape=outs,
        grid=(1,),
        in_specs=[spec(arg) for arg in args],
        out_specs=jax.tree.map(lambda _: VM, outs),
        scratch_shapes=scratch,
        compiler_params=params,
    )(*[arg[0] if isinstance(arg, tuple) else arg for arg in args])


def split(array, axis):
    return array.reshape(lax.axis_size(axis), -1, *array.shape[-2:])


def attend(sent_a, sent_d, layer):
    sent_a, sent_d = split(sent_a, "col"), split(sent_d, "row")
    scratch, sems, outs = [], [], []
    for sent in (sent_a, sent_d):
        count, items, _, width = sent.shape
        outs.append(jax.ShapeDtypeStruct((count, items, HD, width), jnp.bfloat16))
        scratch.append(pltpu.VMEM(sent.shape, jnp.bfloat16))
        sems += [pltpu.SemaphoreType.DMA((items, count))] * 4 + [pltpu.SemaphoreType.DMA]
    for out in outs:
        scratch.append(pltpu.VMEM(out.shape, jnp.bfloat16))
    count = max(sent_a.shape[0], sent_d.shape[0])
    width = max(sent_a.shape[-1], sent_d.shape[-1])
    scratch += [
        pltpu.VMEM((count * width, 2 * HD), jnp.bfloat16),
        pltpu.VMEM((2, count, HD, width), jnp.bfloat16),
        pltpu.VMEM((count, 2 * HD, width), jnp.bfloat16),
        pltpu.VMEM((2, count * width, width), jnp.float32),
        pltpu.VMEM((2, 1, width), jnp.float32),
    ]
    heads = call(
        layer_kernel,
        tuple(outs),
        scratch + sems,
        sent_a,
        sent_d,
        params=pltpu.CompilerParams(collective_id=layer, has_side_effects=True),
    )
    return [array.reshape(-1, *array.shape[-2:]) for array in heads]


def shards(frame, gain_attn, w_qkv, w_out, gain_mlp, w_up, w_down):
    rows, cols, _ = frame.shape
    items_a = rows // SW * HALF
    items_d = cols // SW * HALF
    gain_attn, gain_mlp = gain_attn[:, None], gain_mlp[:, None]
    sent = (
        jax.ShapeDtypeStruct((items_a, 3 * HD, SW * cols), jnp.bfloat16),
        jax.ShapeDtypeStruct((items_d, 3 * HD, SW * rows), jnp.bfloat16),
    )
    tokens = pltpu.VMEM((rows, cols // SW, SW, D), jnp.float32)
    flipped = pltpu.VMEM((3, D, D), jnp.bfloat16)
    shape = jax.ShapeDtypeStruct(frame.shape, jnp.bfloat16)
    state = frame
    sent_a, sent_d = call(first_kernel, sent, [tokens, flipped], frame, (gain_attn, 0), (w_qkv, 0))
    for layer in range(LAYERS):
        heads_a, heads_d = attend(sent_a, sent_d, layer)
        args = (state, heads_a, heads_d, *[(array, layer) for array in (w_out, gain_mlp, w_up, w_down)])
        if layer + 1 < LAYERS:
            state, sent_a, sent_d = call(
                middle_kernel,
                (shape,) + sent,
                [tokens, tokens, flipped],
                *args,
                (gain_attn, layer + 1),
                (w_qkv, layer + 1),
            )
        else:
            state = call(last_kernel, shape, [tokens], *args)
    return state


def solution(mesh):
    placed = (P("row", "col", None), P(), P(), P(), P(), P(), P())
    return jax.shard_map(
        shards, mesh=mesh, in_specs=placed, out_specs=P("row", "col", None), check_vma=False
    )
```

time: 181 us -> 101 us (0.56)
  blocking collectives: 46.6 us -> 0 us
  waiting for transfers between devices: 20.2 us -> 0 us
  starting transfers between devices: 19 us -> 0 us
  Pallas kernels: 84.5 us -> 98.5 us
  local copies, waits for them, and re-layouts: 9.16 us -> 1.87 us
    all_to_all x3 -> x0, blocking collectives: 46.6 us -> none  [exchange(): return lax.all_to_all(split, axis, split_axis=0, concat_axis=0, tiled=True)]
    all_to_all x5 -> x0, waiting for transfers between devices: 20.2 us -> none  [exchange(): return lax.all_to_all(split, axis, split_axis=0, concat_axis=0, tiled=True)]
    all_to_all x5 -> x0, starting transfers between devices: 19 us -> none  [exchange(): return lax.all_to_all(split, axis, split_axis=0, concat_axis=0, tiled=True)]
    pallas_call x7 -> x5, Pallas kernels: 84.5 us -> 98.5 us  [call(): pl.pallas_call(kernel, out_shape=outs, grid=(1,), in_specs=[spec(arg) for...]
    slice x5 -> x0, local copies, waits for them, and re-layouts: 3.54 us -> none  [the longest x1 1.36 us: shards(): gain_attn[layer + 1:layer + 2]]
    unnamed x19 -> x2, local copies, waits for them, and re-layouts: 2.83 us -> 0.01 us
    squeeze x3 -> x0, local copies, waits for them, and re-layouts: 2.8 us -> none  [the longest x1 1.04 us: shards(): w_down[layer]]
    broadcast_in_dim x0 -> x2, local copies, waits for them, and re-layouts: none -> 1.87 us  [shards(): gain_attn, gain_mlp = (gain_attn[:, None], gain_mlp[:, None])]
  transfers between devices with their start and end apart: 5 -> 0, of which waited for: 3 -> 0; matrix products, arithmetic and copies ran while one was open for 2% -> 0% of each run, Pallas kernels for 39% -> 0%
where the time goes in v1:
time: 101 us; the launch traced here: 100 us
  Pallas kernels  98.5 us (98%)
  local copies, waits for them, and re-layouts  1.87 us (2%)
    pallas_call x5, Pallas kernels, call(): pl.pallas_call(kernel, out_shape=outs, grid=(1,), in_specs=[spec(arg) for...  98.5 us

profile of v1, /device:TPU:0, one launch (start us, length us, event | category | flops | bytes accessed | tf_op | source)
XLA Modules:
  0.0 100.4 jit_solution(11181465838052642339)
XLA Ops:
  0.0 0.0 copy-start
  0.0 1.3 %broadcast_in_dim.6.gain_ref.gain = f32[2,1,256]{2,1,0:T(1,128)} reshape(f32[2,256]{1,0:T(2,128)} %param.8) | data formatting | bytes 4096 | tf_op jit(solution)/shard_map/broadcast_in_dim | solution.py:320
  1.3 0.0 copy-done
  1.3 0.6 broadcast_in_dim.7.gain_mlp
  1.9 3.4 %shard_map.73 = (bf16[16,96,256]{2,1,0:T(8,128)(2,1)}, bf16[16,96,256]{2,1,0:T(8,128)(2,1)}) custom-call(bf16[32,32,256]{2,1,0:T(8,128)(2,1)} %x_ref.3, f32[2,1,256]{2,1,0:T(1,128)} %broadcast_in_dim.6.gain_ref.gain, bf16[2,256,768]{2,1,0:T(8,128)(2,1)} %w_ref.3), custom_call_target="tpu_custom_call" | custom-call | tf_op jit(solution)/shard_map/pallas_call | solution.py:271
  5.3 42.4 %shard_map.74 = (bf16[8,2,32,256]{3,2,1,0:T(8,128)(2,1)}, bf16[4,4,32,256]{3,2,1,0:T(8,128)(2,1)}) custom-call(bf16[8,2,96,256]{3,2,1,0:T(8,128)(2,1)} %bitcast.10, bf16[4,4,96,256]{3,2,1,0:T(8,128)(2,1)} %bitcast.11), custom_call_target="tpu_custom_call" | custom-call | tf_op jit(solution)/shard_map/pallas_call | solution.py:271
  47.7 7.3 %shard_map.75 = (bf16[32,32,256]{2,1,0:T(8,128)(2,1)}, bf16[16,96,256]{2,1,0:T(8,128)(2,1)}, bf16[16,96,256]{2,1,0:T(8,128)(2,1)}) custom-call(bf16[32,32,256]{2,1,0:T(8,128)(2,1)} %x_ref.3, bf16[16,32,256]{2,1,0:T(8,128)(2,1)} %bitcast.12, bf16[16,32,256]{2,1,0:T(8,128)(2,1)} %bitcast.13, bf16[2,256,256]{2,1,0:T(8,128)(2,1)} %w_out.3, ...), custom_call_target="tpu_custom_call" | custom-call | tf_op jit(solution)/shard_map/pallas_call | solution.py:271
  54.9 40.1 %shard_map.76 = (bf16[8,2,32,256]{3,2,1,0:T(8,128)(2,1)}, bf16[4,4,32,256]{3,2,1,0:T(8,128)(2,1)}) custom-call(bf16[8,2,96,256]{3,2,1,0:T(8,128)(2,1)} %bitcast.8, bf16[4,4,96,256]{3,2,1,0:T(8,128)(2,1)} %bitcast.9), custom_call_target="tpu_custom_call" | custom-call | tf_op jit(solution)/shard_map/pallas_call | solution.py:271
  95.0 5.3 %shard_map.77 = bf16[32,32,256]{2,1,0:T(8,128)(2,1)} custom-call(bf16[32,32,256]{2,1,0:T(8,128)(2,1)} %get-tuple-element.18.x_ref, bf16[16,32,256]{2,1,0:T(8,128)(2,1)} %bitcast.14, bf16[16,32,256]{2,1,0:T(8,128)(2,1)} %bitcast.15, bf16[2,256,256]{2,1,0:T(8,128)(2,1)} %w_out.3, f32[2,1,256]{2,1,0:T(1,128)} %broadcast_in_dim.7.gain_mlp, ...), custom_call_target="tpu_custom_call" | custom-call | tf_op jit(solution)/shard_map/pallas_call | solution.py:271
Async XLA Ops:
  0.0 1.3 %copy-start = (f32[2,256]{1,0:T(2,128)S(1)}, f32[2,256]{1,0:T(2,128)}, u32[]{:S(2)}) copy-start(f32[2,256]{1,0:T(2,128)} %param.11) | copy-start | bytes 6148

commit v2 on v1

--- a/solution.py
+++ b/solution.py
@@ -49,16 +49,16 @@
         emit(normed[band * SW : (band + 1) * SW], 0, sent_a, band)
 
 
-def first_kernel(x_ref, gain_ref, w_ref, sent_a, sent_d, normed, wt):
+def first_kernel(layer, x_ref, gain_ref, w_ref, sent_a, sent_d, normed, wt):
     rows, cols, _ = x_ref.shape
     for band in range(rows // SW):
         part = slice(band * SW, (band + 1) * SW)
         floats = x_ref[part].reshape(-1, D).astype(jnp.float32)
-        normed[part] = normalize(floats, gain_ref[...]).reshape(SW, cols // SW, SW, D)
+        normed[part] = normalize(floats, gain_ref[layer : layer + 1]).reshape(SW, cols // SW, SW, D)
     project(normed, w_ref, sent_a, sent_d, wt)
 
 
-def rest(x_ref, heads_a, heads_d, w_out, gain_mlp, w_up, w_down, y_ref, mixed, normed, gain):
+def rest(layer, x_ref, heads_a, heads_d, w_out, gain_mlp, w_up, w_down, y_ref, mixed, normed, gain):
     rows, cols, _ = x_ref.shape
     bands = cols // SW
     flip = (((0,), (0,)), ((), ()))
@@ -71,25 +71,25 @@
         heads = heads_a[band * HALF : (band + 1) * HALF].reshape(HALF * HD, -1)
         part = lax.dot_general(heads, w_out[: HALF * HD], flip, preferred_element_type=jnp.float32)
         total = x_ref[here].reshape(-1, D).astype(jnp.float32) + (part + mixed[here].reshape(-1, D))
-        normed2 = normalize(total, gain_mlp[...]).astype(jnp.bfloat16)
+        normed2 = normalize(total, gain_mlp[layer : layer + 1]).astype(jnp.bfloat16)
         up = jnp.dot(normed2, w_up[...], preferred_element_type=jnp.float32)
         hidden = jax.nn.gelu(up, approximate=True).astype(jnp.bfloat16)
         final = total + jnp.dot(hidden, w_down[...], preferred_element_type=jnp.float32)
         final = final.astype(jnp.bfloat16)
         y_ref[here] = final.reshape(SW, cols, D)
         if normed is not None:
-            normed[here] = normalize(final.astype(jnp.float32), gain[...]).reshape(SW, bands, SW, D)
+            normed[here] = normalize(final.astype(jnp.float32), gain[layer + 1 : layer + 2]).reshape(SW, bands, SW, D)
 
 
 def middle_kernel(
-    x_ref, heads_a, heads_d, w_out, gain_mlp, w_up, w_down, gain, w_ref, y_ref, sent_a, sent_d, mixed, normed, wt
+    layer, x_ref, heads_a, heads_d, w_out, gain_mlp, w_up, w_down, gain, w_ref, y_ref, sent_a, sent_d, mixed, normed, wt
 ):
-    rest(x_ref, heads_a, heads_d, w_out, gain_mlp, w_up, w_down, y_ref, mixed, normed, gain)
+    rest(layer, x_ref, heads_a, heads_d, w_out, gain_mlp, w_up, w_down, y_ref, mixed, normed, gain)
     project(normed, w_ref, sent_a, sent_d, wt)
 
 
-def last_kernel(x_ref, heads_a, heads_d, w_out, gain_mlp, w_up, w_down, y_ref, mixed):
-    rest(x_ref, heads_a, heads_d, w_out, gain_mlp, w_up, w_down, y_ref, mixed, None, None)
+def last_kernel(layer, x_ref, heads_a, heads_d, w_out, gain_mlp, w_up, w_down, y_ref, mixed):
+    rest(layer, x_ref, heads_a, heads_d, w_out, gain_mlp, w_up, w_down, y_ref, mixed, None, None)
 
 
 def wrap(index, count):
@@ -148,31 +148,34 @@
             self.keys[src * self.width : (src + 1) * self.width] = jnp.concatenate([k, k], axis=0).T
             self.vals[slot, src] = self.got[src, item, 2 * HD :]
 
-    def score(self, unit):
-        slot = lax.rem(unit, 2)
-        q = self.queries[lax.rem(unit, self.count)]
-        tops = []
-        for src in range(self.count):
-            here = slice(src * self.width, (src + 1) * self.width)
-            scores = jnp.dot(self.keys[here], q, preferred_element_type=jnp.float32)
-            self.board[slot, here] = scores
-            tops.append(jnp.max(scores.reshape(-1, 8, self.width), axis=0))
-        self.tops[slot] = jnp.max(functools.reduce(jnp.maximum, tops), axis=0, keepdims=True)
-
-    def finish(self, unit):
-        slot = lax.rem(unit, 2)
-        item, block = unit // self.count, lax.rem(unit, self.count)
-        top = self.tops[slot]
-        sums, total = 0.0, 0.0
-        for src in range(self.count):
-            here = slice(src * self.width, (src + 1) * self.width)
-            probs = jnp.exp2(self.board[slot, here] - top)
-            sums += jnp.sum(probs.reshape(-1, 8, self.width), axis=0)
-            total += jnp.dot(
-                self.vals[lax.rem(item, 2), src], probs.astype(jnp.bfloat16), preferred_element_type=jnp.float32
-            )
-        result = (total / jnp.sum(sums, axis=0, keepdims=True)).astype(jnp.bfloat16)
-        self.outs[block, item] = result
+    def step(self, after, unit):
+        count, width = self.count, self.width
+        if after is not None:
+            after, odd = after
+            q = self.queries[lax.rem(after, count)]
+            tops = []
+        if unit is not None:
+            unit, even = unit
+            item, block = unit // count, lax.rem(unit, count)
+            slot = lax.rem(item, 2)
+            top = self.tops[even][...]
+            sums, total = 0.0, 0.0
+        for src in range(count):
+            here = slice(src * width, (src + 1) * width)
+            if after is not None:
+                scores = jnp.dot(self.keys[here], q, preferred_element_type=jnp.float32)
+                self.board[odd][here] = scores
+                tops.append(jnp.max(scores.reshape(-1, 8, width), axis=0))
+            if unit is not None:
+                probs = jnp.exp2(self.board[even][here] - top)
+                sums += jnp.sum(probs.reshape(-1, 8, width), axis=0)
+                total += jnp.dot(
+                    self.vals[slot, src], probs.astype(jnp.bfloat16), preferred_element_type=jnp.float32
+                )
+        if after is not None:
+            self.tops[odd][...] = jnp.max(functools.reduce(jnp.maximum, tops), axis=0, keepdims=True)
+        if unit is not None:
+            self.outs[block, item] = (total / jnp.sum(sums, axis=0, keepdims=True)).astype(jnp.bfloat16)
 
     def deliver(self, unit):
         item, block = unit // self.count, lax.rem(unit, self.count)
@@ -186,28 +189,34 @@
             self.outward(item, block).start()
 
     def run(self):
+        units = self.units
+        assert self.count % 2 == 0
         self.prepare(0)
-        self.score(0)
-
-        @pl.loop(0, self.units - 1)
+        self.step((0, 0), None)
+
+        @pl.loop(0, units - 2, step=2)
         def _(unit):
-            after = unit + 1
+            self.step((unit + 1, 1), (unit, 0))
+
+            @pl.when(unit > 0)
+            def _():
+                self.deliver(unit - 1)
+
+            after = unit + 2
 
             @pl.when(lax.rem(after, self.count) == 0)
             def _():
                 self.prepare(after // self.count)
 
-            self.score(after)
-            self.finish(unit)
-
-            @pl.when(unit > 0)
-            def _():
-                self.deliver(unit - 1)
-
-        self.finish(self.units - 1)
-        if self.units > 1:
-            self.deliver(self.units - 2)
-        self.deliver(self.units - 1)
+            self.step((after, 0), (unit + 1, 1))
+            self.deliver(unit)
+
+        self.step((units - 1, 1), (units - 2, 0))
+        if units > 2:
+            self.deliver(units - 3)
+        self.step(None, (units - 1, 1))
+        self.deliver(units - 2)
+        self.deliver(units - 1)
 
     def drain(self):
         for item in range(self.items):
@@ -217,7 +226,7 @@
 
 
 def layer_kernel(
-    sent_a, sent_d, heads_a, heads_d, got_a, got_d, outs_a, outs_d, keys, vals, queries, board, tops, *sems
+    sent_a, sent_d, heads_a, heads_d, got_a, got_d, outs_a, outs_d, keys, vals, queries, even, odd, even_top, odd_top, *sems
 ):
     def stream(axis, sent, heads, got, outs, sems):
         count, _, _, width = got.shape
@@ -230,8 +239,8 @@
             keys.at[: count * width],
             vals.at[:, :count],
             queries.at[:count],
-            board.at[:, : count * width],
-            tops,
+            (even.at[: count * width], odd.at[: count * width]),
+            (even_top, odd_top),
             sems,
         )
 
@@ -299,8 +308,10 @@
         pltpu.VMEM((count * width, 2 * HD), jnp.bfloat16),
         pltpu.VMEM((2, count, HD, width), jnp.bfloat16),
         pltpu.VMEM((count, 2 * HD, width), jnp.bfloat16),
-        pltpu.VMEM((2, count * width, width), jnp.float32),
-        pltpu.VMEM((2, 1, width), jnp.float32),
+        pltpu.VMEM((count * width, width), jnp.float32),
+        pltpu.VMEM((count * width, width), jnp.float32),
+        pltpu.VMEM((1, width), jnp.float32),
+        pltpu.VMEM((1, width), jnp.float32),
     ]
     heads = call(
         layer_kernel,
@@ -317,7 +328,6 @@
     rows, cols, _ = frame.shape
     items_a = rows // SW * HALF
     items_d = cols // SW * HALF
-    gain_attn, gain_mlp = gain_attn[:, None], gain_mlp[:, None]
     sent = (
         jax.ShapeDtypeStruct((items_a, 3 * HD, SW * cols), jnp.bfloat16),
         jax.ShapeDtypeStruct((items_d, 3 * HD, SW * rows), jnp.bfloat16),
@@ -326,21 +336,21 @@
     flipped = pltpu.VMEM((3, D, D), jnp.bfloat16)
     shape = jax.ShapeDtypeStruct(frame.shape, jnp.bfloat16)
     state = frame
-    sent_a, sent_d = call(first_kernel, sent, [tokens, flipped], frame, (gain_attn, 0), (w_qkv, 0))
+    sent_a, sent_d = call(functools.partial(first_kernel, 0), sent, [tokens, flipped], frame, gain_attn, (w_qkv, 0))
     for layer in range(LAYERS):
         heads_a, heads_d = attend(sent_a, sent_d, layer)
-        args = (state, heads_a, heads_d, *[(array, layer) for array in (w_out, gain_mlp, w_up, w_down)])
+        args = (state, heads_a, heads_d, (w_out, layer), gain_mlp, (w_up, layer), (w_down, layer))
         if layer + 1 < LAYERS:
             state, sent_a, sent_d = call(
-                middle_kernel,
+                functools.partial(middle_kernel, layer),
                 (shape,) + sent,
                 [tokens, tokens, flipped],
                 *args,
-                (gain_attn, layer + 1),
+                gain_attn,
                 (w_qkv, layer + 1),
             )
         else:
-            state = call(last_kernel, shape, [tokens], *args)
+            state = call(functools.partial(last_kernel, layer), shape, [tokens], *args)
     return state
 
 

time: 101 us -> 86 us (0.85)
  Pallas kernels: 98.5 us -> 85.7 us
  local copies, waits for them, and re-layouts: 1.87 us -> 0 us
    pallas_call x5, Pallas kernels: 98.5 us -> 85.7 us  [call(): pl.pallas_call(kernel, out_shape=outs, grid=(1,), in_specs=[spec(arg) for...]
    broadcast_in_dim x2 -> x0, local copies, waits for them, and re-layouts: 1.87 us -> none  [shards(): gain_attn, gain_mlp = (gain_attn[:, None], gain_mlp[:, None])]
where the time goes in v2:
time: 86 us; the launch traced here: 85.7 us
  Pallas kernels  85.7 us (100%)
    pallas_call x5, Pallas kernels, call(): pl.pallas_call(kernel, out_shape=outs, grid=(1,), in_specs=[spec(arg) for...  85.7 us

profile of v2, /device:TPU:0, one launch (start us, length us, event | category | flops | bytes accessed | tf_op | source)
XLA Modules:
  0.0 85.7 jit_solution(5454134444289729898)
XLA Ops:
  0.0 3.4 %shard_map.73 = (bf16[16,96,256]{2,1,0:T(8,128)(2,1)}, bf16[16,96,256]{2,1,0:T(8,128)(2,1)}) custom-call(bf16[32,32,256]{2,1,0:T(8,128)(2,1)} %x_ref.3, f32[2,256]{1,0:T(2,128)} %gain.1, bf16[2,256,768]{2,1,0:T(8,128)(2,1)} %w_ref.3), custom_call_target="tpu_custom_call" | custom-call | tf_op jit(solution)/shard_map/pallas_call | solution.py:280
  3.4 36.1 %shard_map.74 = (bf16[8,2,32,256]{3,2,1,0:T(8,128)(2,1)}, bf16[4,4,32,256]{3,2,1,0:T(8,128)(2,1)}) custom-call(bf16[8,2,96,256]{3,2,1,0:T(8,128)(2,1)} %bitcast.10, bf16[4,4,96,256]{3,2,1,0:T(8,128)(2,1)} %bitcast.11), custom_call_target="tpu_custom_call" | custom-call | tf_op jit(solution)/shard_map/pallas_call | solution.py:280
  39.5 7.3 %shard_map.75 = (bf16[32,32,256]{2,1,0:T(8,128)(2,1)}, bf16[16,96,256]{2,1,0:T(8,128)(2,1)}, bf16[16,96,256]{2,1,0:T(8,128)(2,1)}) custom-call(bf16[32,32,256]{2,1,0:T(8,128)(2,1)} %x_ref.3, bf16[16,32,256]{2,1,0:T(8,128)(2,1)} %bitcast.12, bf16[16,32,256]{2,1,0:T(8,128)(2,1)} %bitcast.13, bf16[2,256,256]{2,1,0:T(8,128)(2,1)} %w_out.3, f32[2,256]{1,0:T(2,128)} %gain_mlp.3, ...), custom_call_target="tpu_custom_call" | custom-call | tf_op jit(solution)/shard_map/pallas_call | solution.py:280
  46.8 33.6 %shard_map.76 = (bf16[8,2,32,256]{3,2,1,0:T(8,128)(2,1)}, bf16[4,4,32,256]{3,2,1,0:T(8,128)(2,1)}) custom-call(bf16[8,2,96,256]{3,2,1,0:T(8,128)(2,1)} %bitcast.8, bf16[4,4,96,256]{3,2,1,0:T(8,128)(2,1)} %bitcast.9), custom_call_target="tpu_custom_call" | custom-call | tf_op jit(solution)/shard_map/pallas_call | solution.py:280
  80.4 5.3 %shard_map.77 = bf16[32,32,256]{2,1,0:T(8,128)(2,1)} custom-call(bf16[32,32,256]{2,1,0:T(8,128)(2,1)} %get-tuple-element.18.x_ref, bf16[16,32,256]{2,1,0:T(8,128)(2,1)} %bitcast.14, bf16[16,32,256]{2,1,0:T(8,128)(2,1)} %bitcast.15, bf16[2,256,256]{2,1,0:T(8,128)(2,1)} %w_out.3, f32[2,256]{1,0:T(2,128)} %gain_mlp.3, bf16[2,256,1024]{2,1,0:T(8,128)(2,1)} %w_up.3, ...), custom_call_target="tpu_custom_call" | custom-call | tf_op jit(solution)/shard_map/pallas_call | solution.py:280

commit v3 on v2

--- a/solution.py
+++ b/solution.py
@@ -15,6 +15,8 @@
 HALF = HEADS // 2
 HD = D // HEADS
 EPS = 1e-05
+UNROLL = 4
+LAG = 2
 SCALE = HD**-0.5 * math.log2(math.e)
 
 
@@ -143,16 +145,17 @@
             q = self.got[src, item, :HD].astype(jnp.float32) * SCALE
             high = q.astype(jnp.bfloat16)
             low = (q - high.astype(jnp.float32)).astype(jnp.bfloat16)
-            self.queries[src] = jnp.concatenate([high, low], axis=0)
+            self.queries[slot, src] = jnp.concatenate([high, low], axis=0)
             k = self.got[src, item, HD : 2 * HD]
-            self.keys[src * self.width : (src + 1) * self.width] = jnp.concatenate([k, k], axis=0).T
+            self.keys[slot, src * self.width : (src + 1) * self.width] = jnp.concatenate([k, k], axis=0).T
             self.vals[slot, src] = self.got[src, item, 2 * HD :]
 
     def step(self, after, unit):
         count, width = self.count, self.width
         if after is not None:
             after, odd = after
-            q = self.queries[lax.rem(after, count)]
+            fresh = lax.rem(after // count, 2)
+            q = self.queries[fresh, lax.rem(after, count)]
             tops = []
         if unit is not None:
             unit, even = unit
@@ -163,7 +166,7 @@
         for src in range(count):
             here = slice(src * width, (src + 1) * width)
             if after is not None:
-                scores = jnp.dot(self.keys[here], q, preferred_element_type=jnp.float32)
+                scores = jnp.dot(self.keys[fresh, here], q, preferred_element_type=jnp.float32)
                 self.board[odd][here] = scores
                 tops.append(jnp.max(scores.reshape(-1, 8, width), axis=0))
             if unit is not None:
@@ -189,34 +192,31 @@
             self.outward(item, block).start()
 
     def run(self):
-        units = self.units
-        assert self.count % 2 == 0
+        unroll = UNROLL
+        assert self.count % unroll == 0
         self.prepare(0)
-        self.step((0, 0), None)
-
-        @pl.loop(0, units - 2, step=2)
+        for ahead in range(LAG):
+            self.step((ahead, ahead), None)
+
+        @pl.loop(0, self.units, step=unroll)
         def _(unit):
-            self.step((unit + 1, 1), (unit, 0))
+            after = unit + unroll
+
+            @pl.when(jnp.logical_and(lax.rem(after, self.count) == 0, after < self.units))
+            def _():
+                self.prepare(after // self.count)
+
+            for ahead in range(unroll):
+                self.step((unit + ahead + LAG, (ahead + LAG) % unroll), (unit + ahead, ahead))
 
             @pl.when(unit > 0)
             def _():
                 self.deliver(unit - 1)
 
-            after = unit + 2
-
-            @pl.when(lax.rem(after, self.count) == 0)
-            def _():
-                self.prepare(after // self.count)
-
-            self.step((after, 0), (unit + 1, 1))
-            self.deliver(unit)
-
-        self.step((units - 1, 1), (units - 2, 0))
-        if units > 2:
-            self.deliver(units - 3)
-        self.step(None, (units - 1, 1))
-        self.deliver(units - 2)
-        self.deliver(units - 1)
+            for ahead in range(unroll - 1):
+                self.deliver(unit + ahead)
+
+        self.deliver(self.units - 1)
 
     def drain(self):
         for item in range(self.items):
@@ -226,8 +226,10 @@
 
 
 def layer_kernel(
-    sent_a, sent_d, heads_a, heads_d, got_a, got_d, outs_a, outs_d, keys, vals, queries, even, odd, even_top, odd_top, *sems
+    sent_a, sent_d, heads_a, heads_d, got_a, got_d, outs_a, outs_d, keys, vals, queries, *rest
 ):
+    boards, tops, sems = rest[:UNROLL], rest[UNROLL : 2 * UNROLL], rest[2 * UNROLL :]
+
     def stream(axis, sent, heads, got, outs, sems):
         count, _, _, width = got.shape
         return Stream(
@@ -236,11 +238,11 @@
             heads,
             got,
             outs,
-            keys.at[: count * width],
+            keys.at[:, : count * width],
             vals.at[:, :count],
-            queries.at[:count],
-            (even.at[: count * width], odd.at[: count * width]),
-            (even_top, odd_top),
+            queries.at[:, :count],
+            [board.at[: count * width] for board in boards],
+            tops,
             sems,
         )
 
@@ -305,14 +307,12 @@
     count = max(sent_a.shape[0], sent_d.shape[0])
     width = max(sent_a.shape[-1], sent_d.shape[-1])
     scratch += [
-        pltpu.VMEM((count * width, 2 * HD), jnp.bfloat16),
+        pltpu.VMEM((2, count * width, 2 * HD), jnp.bfloat16),
         pltpu.VMEM((2, count, HD, width), jnp.bfloat16),
-        pltpu.VMEM((count, 2 * HD, width), jnp.bfloat16),
-        pltpu.VMEM((count * width, width), jnp.float32),
-        pltpu.VMEM((count * width, width), jnp.float32),
-        pltpu.VMEM((1, width), jnp.float32),
-        pltpu.VMEM((1, width), jnp.float32),
+        pltpu.VMEM((2, count, 2 * HD, width), jnp.bfloat16),
     ]
+    scratch += [pltpu.VMEM((count * width, width), jnp.float32)] * UNROLL
+    scratch += [pltpu.VMEM((1, width), jnp.float32)] * UNROLL
     heads = call(
         layer_kernel,
         tuple(outs),

time: 86 us -> 87.6 us (1.019)
  Pallas kernels: 85.7 us -> 87.3 us
    pallas_call x5, Pallas kernels: 85.7 us -> 87.3 us  [call(): pl.pallas_call(kernel, out_shape=outs, grid=(1,), in_specs=[spec(arg) for...]
where the time goes in v3:
time: 87.6 us; the launch traced here: 87.4 us
  Pallas kernels  87.3 us (100%)
    pallas_call x5, Pallas kernels, call(): pl.pallas_call(kernel, out_shape=outs, grid=(1,), in_specs=[spec(arg) for...  87.3 us

profile of v3, /device:TPU:0, one launch (start us, length us, event | category | flops | bytes accessed | tf_op | source)
XLA Modules:
  0.0 87.4 jit_solution(7800646941652880195)
XLA Ops:
  0.0 3.4 %shard_map.73 = (bf16[16,96,256]{2,1,0:T(8,128)(2,1)}, bf16[16,96,256]{2,1,0:T(8,128)(2,1)}) custom-call(bf16[32,32,256]{2,1,0:T(8,128)(2,1)} %x_ref.3, f32[2,256]{1,0:T(2,128)} %gain.1, bf16[2,256,768]{2,1,0:T(8,128)(2,1)} %w_ref.3), custom_call_target="tpu_custom_call" | custom-call | tf_op jit(solution)/shard_map/pallas_call | solution.py:282
  3.4 37.4 %shard_map.74 = (bf16[8,2,32,256]{3,2,1,0:T(8,128)(2,1)}, bf16[4,4,32,256]{3,2,1,0:T(8,128)(2,1)}) custom-call(bf16[8,2,96,256]{3,2,1,0:T(8,128)(2,1)} %bitcast.10, bf16[4,4,96,256]{3,2,1,0:T(8,128)(2,1)} %bitcast.11), custom_call_target="tpu_custom_call" | custom-call | tf_op jit(solution)/shard_map/pallas_call | solution.py:282
  40.8 7.3 %shard_map.75 = (bf16[32,32,256]{2,1,0:T(8,128)(2,1)}, bf16[16,96,256]{2,1,0:T(8,128)(2,1)}, bf16[16,96,256]{2,1,0:T(8,128)(2,1)}) custom-call(bf16[32,32,256]{2,1,0:T(8,128)(2,1)} %x_ref.3, bf16[16,32,256]{2,1,0:T(8,128)(2,1)} %bitcast.12, bf16[16,32,256]{2,1,0:T(8,128)(2,1)} %bitcast.13, bf16[2,256,256]{2,1,0:T(8,128)(2,1)} %w_out.3, f32[2,256]{1,0:T(2,128)} %gain_mlp.3, ...), custom_call_target="tpu_custom_call" | custom-call | tf_op jit(solution)/shard_map/pallas_call | solution.py:282
  48.1 34.0 %shard_map.76 = (bf16[8,2,32,256]{3,2,1,0:T(8,128)(2,1)}, bf16[4,4,32,256]{3,2,1,0:T(8,128)(2,1)}) custom-call(bf16[8,2,96,256]{3,2,1,0:T(8,128)(2,1)} %bitcast.8, bf16[4,4,96,256]{3,2,1,0:T(8,128)(2,1)} %bitcast.9), custom_call_target="tpu_custom_call" | custom-call | tf_op jit(solution)/shard_map/pallas_call | solution.py:282
  82.0 5.3 %shard_map.77 = bf16[32,32,256]{2,1,0:T(8,128)(2,1)} custom-call(bf16[32,32,256]{2,1,0:T(8,128)(2,1)} %get-tuple-element.18.x_ref, bf16[16,32,256]{2,1,0:T(8,128)(2,1)} %bitcast.14, bf16[16,32,256]{2,1,0:T(8,128)(2,1)} %bitcast.15, bf16[2,256,256]{2,1,0:T(8,128)(2,1)} %w_out.3, f32[2,256]{1,0:T(2,128)} %gain_mlp.3, bf16[2,256,1024]{2,1,0:T(8,128)(2,1)} %w_up.3, ...), custom_call_target="tpu_custom_call" | custom-call | tf_op jit(solution)/shard_map/pallas_call | solution.py:282

commit v4 on v3

--- a/solution.py
+++ b/solution.py
@@ -206,15 +206,16 @@
             def _():
                 self.prepare(after // self.count)
 
+            @pl.when(unit > 0)
+            def _():
+                self.outward((unit - 1) // self.count, lax.rem(unit - 1, self.count)).start()
+
+            item, block = unit // self.count, lax.rem(unit, self.count)
             for ahead in range(unroll):
                 self.step((unit + ahead + LAG, (ahead + LAG) % unroll), (unit + ahead, ahead))
-
-            @pl.when(unit > 0)
-            def _():
-                self.deliver(unit - 1)
-
-            for ahead in range(unroll - 1):
-                self.deliver(unit + ahead)
+                if ahead > 1:
+                    self.outward(item, block + ahead - 1).start()
+            self.deliver(unit)
 
         self.deliver(self.units - 1)
 

time: 87.6 us -> 87.9 us (level)
  no operation moved by 1% of the time
where the time goes in v4:
time: 87.9 us; the launch traced here: 87.7 us
  Pallas kernels  87.7 us (100%)
    pallas_call x5, Pallas kernels, call(): pl.pallas_call(kernel, out_shape=outs, grid=(1,), in_specs=[spec(arg) for...  87.7 us

profile of v4, /device:TPU:0, one launch (start us, length us, event | category | flops | bytes accessed | tf_op | source)
XLA Modules:
  0.0 87.7 jit_solution(7390068545937357916)
XLA Ops:
  0.0 3.4 %shard_map.73 = (bf16[16,96,256]{2,1,0:T(8,128)(2,1)}, bf16[16,96,256]{2,1,0:T(8,128)(2,1)}) custom-call(bf16[32,32,256]{2,1,0:T(8,128)(2,1)} %x_ref.3, f32[2,256]{1,0:T(2,128)} %gain.1, bf16[2,256,768]{2,1,0:T(8,128)(2,1)} %w_ref.3), custom_call_target="tpu_custom_call" | custom-call | tf_op jit(solution)/shard_map/pallas_call | solution.py:283
  3.4 37.2 %shard_map.74 = (bf16[8,2,32,256]{3,2,1,0:T(8,128)(2,1)}, bf16[4,4,32,256]{3,2,1,0:T(8,128)(2,1)}) custom-call(bf16[8,2,96,256]{3,2,1,0:T(8,128)(2,1)} %bitcast.10, bf16[4,4,96,256]{3,2,1,0:T(8,128)(2,1)} %bitcast.11), custom_call_target="tpu_custom_call" | custom-call | tf_op jit(solution)/shard_map/pallas_call | solution.py:283
  40.6 7.3 %shard_map.75 = (bf16[32,32,256]{2,1,0:T(8,128)(2,1)}, bf16[16,96,256]{2,1,0:T(8,128)(2,1)}, bf16[16,96,256]{2,1,0:T(8,128)(2,1)}) custom-call(bf16[32,32,256]{2,1,0:T(8,128)(2,1)} %x_ref.3, bf16[16,32,256]{2,1,0:T(8,128)(2,1)} %bitcast.12, bf16[16,32,256]{2,1,0:T(8,128)(2,1)} %bitcast.13, bf16[2,256,256]{2,1,0:T(8,128)(2,1)} %w_out.3, f32[2,256]{1,0:T(2,128)} %gain_mlp.3, ...), custom_call_target="tpu_custom_call" | custom-call | tf_op jit(solution)/shard_map/pallas_call | solution.py:283
  47.8 34.5 %shard_map.76 = (bf16[8,2,32,256]{3,2,1,0:T(8,128)(2,1)}, bf16[4,4,32,256]{3,2,1,0:T(8,128)(2,1)}) custom-call(bf16[8,2,96,256]{3,2,1,0:T(8,128)(2,1)} %bitcast.8, bf16[4,4,96,256]{3,2,1,0:T(8,128)(2,1)} %bitcast.9), custom_call_target="tpu_custom_call" | custom-call | tf_op jit(solution)/shard_map/pallas_call | solution.py:283
  82.4 5.3 %shard_map.77 = bf16[32,32,256]{2,1,0:T(8,128)(2,1)} custom-call(bf16[32,32,256]{2,1,0:T(8,128)(2,1)} %get-tuple-element.18.x_ref, bf16[16,32,256]{2,1,0:T(8,128)(2,1)} %bitcast.14, bf16[16,32,256]{2,1,0:T(8,128)(2,1)} %bitcast.15, bf16[2,256,256]{2,1,0:T(8,128)(2,1)} %w_out.3, f32[2,256]{1,0:T(2,128)} %gain_mlp.3, bf16[2,256,1024]{2,1,0:T(8,128)(2,1)} %w_up.3, ...), custom_call_target="tpu_custom_call" | custom-call | tf_op jit(solution)/shard_map/pallas_call | solution.py:283
